TPU v7x, 256 devices: a whole 4x4x8 slice. The times are simulated.
256 devices in a mesh: grp: 8 (over z), blk: 32 (over x, y, core).
Axes of the slice: x: 4, y: 4, z: 8, core: 2. Of those that a mesh axis runs over, the one named last changes fastest.
Arguments:
- tokens: bfloat16 [8, 4096, 1024], P('grp', 'blk'), may hold values from -40 to 40
- lengths: int32 [8, 16], P('grp'), may hold values from 1 to 2176, 4096 in all within a row
- owners: int32 [8], P('grp'), may hold values from 0 to 7
- prefix_cache: bfloat16 [8, 2048, 1024], P('grp', 'blk'), may hold values from -52 to 52
- routes: int32 [8, 4096, 2], P('grp', 'blk'), may hold values from 0 to 7, all different within a row; in each aligned block of 128 rows (0 to 127, 128 to 255, ..., all dimensions but the last counted through in order) at most 40 rows name the same one
- gates: float32 [8, 4096, 2], P('grp', 'blk'), may hold values from 0.2 to 1
- attn_gain: float32 [1024], replicated, may hold values from 0.5 to 1.5
- w_query: bfloat16 [1024, 512], replicated, may hold values from -0.5 to 0.5
- w_keyval: bfloat16 [1024, 1024], replicated, may hold values from -0.1875 to 0.1875
- w_out: bfloat16 [512, 1024], replicated, may hold values from -0.25 to 0.25
- moe_gain: float32 [1024], replicated, may hold values from 0.5 to 1.5
- w_gate: bfloat16 [32, 1024, 704], P('blk'), may hold values from -0.1875 to 0.1875
- w_up: bfloat16 [32, 1024, 704], P('blk'), may hold values from -0.1875 to 0.1875
- w_down: bfloat16 [32, 704, 1024], P('blk'), may hold values from -0.109375 to 0.109375
- final_gain: float32 [1024], replicated, may hold values from 0.5 to 1.5
- unembed: bfloat16 [1024, 32128], P(None, 'blk'), may hold values from -0.5 to 0.5
Outputs:
- hidden: bfloat16 [8, 4096, 1024], P('grp', 'blk')
- suffix_cache: bfloat16 [8, 4096, 1024], P('grp', 'blk')
- request_norm: float32 [8, 16], P('grp')
- greatest: float32 [8, 16], P('grp')
Inputs may be any that keep to these rules, and one draw needn't show every extreme that they name: In each group the lengths sum to 4096, and the longest request has exactly 2176 tokens. `routes`: the two experts of a token differ. Within the 128 rows of one device no expert is named more than 40 times, and in some device's rows an expert is named exactly 40 times.
All inputs are finite; a program needn't handle non-finite values.
Results may differ from a plain program's by a relative error of at most 0.0052.
The roundings to bfloat16 on the way count: a program that leaves them out, or rounds other values in their place, can miss the bound.
Values may be sent and summed in bfloat16 or wider, within the bound.
No kernel may reach another device: no remote copies, remote signals or barrier semaphores. Data moves between devices by JAX's collectives and lax.ppermute only.
A program may use at most 128 MiB of HBM per device.

v0:
```python
import jax
import jax.numpy as jnp
from jax import lax
from jax.sharding import PartitionSpec as P

HEADS = 8
EXPERTS = 8
CAP = 40
epsilon = 1e-06
neg_big = -1e30


def rms_scale(values, gain_vector):
    values = values.astype(jnp.float32)
    return (
        values
        * lax.rsqrt(jnp.mean(values * values, axis=-1, keepdims=True) + epsilon)
        * gain_vector
    )


def request_of(positions, end_points):
    return jnp.sum((positions[:, None] >= end_points[None, :]).astype(jnp.int32), axis=1)


def slot_targets(block_routes):
    flat_routes = block_routes.reshape(-1)
    onehot = (flat_routes[:, None] == jnp.arange(EXPERTS, dtype=jnp.int32)[None, :]).astype(
        jnp.int32
    )
    before = jnp.cumsum(onehot, axis=0) - onehot
    slot_index = jnp.sum(before * onehot, axis=1)
    return (flat_routes * CAP + slot_index).reshape(block_routes.shape)


def dispatch_matrix(targets):
    slot_ids = jnp.arange(EXPERTS * CAP, dtype=jnp.int32)
    matches = (targets[:, 0][None, :] == slot_ids[:, None]) | (
        targets[:, 1][None, :] == slot_ids[:, None]
    )
    return matches.astype(jnp.bfloat16)


def attend_piece(carry_state, query_set, key_part, key_req, key_pos, masked):
    context_sum, row_max, row_total = carry_state
    queries, query_req, query_pos = query_set
    head_count = row_max.shape[0]
    piece_rows = key_part.shape[0]
    attn_width = key_part.shape[1] // 2
    head_size = attn_width // head_count
    key_heads = key_part[:, :attn_width].reshape(piece_rows, head_count, head_size)
    value_heads = key_part[:, attn_width:].reshape(piece_rows, head_count, head_size)
    query_heads = queries.reshape(queries.shape[0], head_count, head_size)
    scores = jnp.einsum(
        "qhd,khd->hqk", query_heads, key_heads, preferred_element_type=jnp.float32
    ) * head_size ** (-0.5)
    if masked:
        allowed = (query_req[:, None] == key_req[None, :]) & (
            key_pos[None, :] <= query_pos[:, None]
        )
        scores = jnp.where(allowed[None], scores, neg_big)
    new_max = jnp.maximum(row_max, jnp.max(scores, axis=-1))
    shrink = jnp.exp(row_max - new_max)
    probs_full = jnp.exp(scores - new_max[..., None])
    row_total = row_total * shrink + jnp.sum(probs_full, axis=-1)
    context_sum = context_sum * shrink[..., None] + jnp.einsum(
        "hqk,khd->hqd",
        probs_full.astype(jnp.bfloat16),
        value_heads,
        preferred_element_type=jnp.float32,
    )
    return (context_sum, new_max, row_total)


def fold_sets(states, query_sets, key_part, key_req, key_pos, masked, request_ends):
    results = []
    for state_one, set_one in zip(states, query_sets):
        if masked:
            first_req = set_one[1][0]
            earliest = jnp.where(first_req > 0, request_ends[jnp.maximum(first_req - 1, 0)], 0)
            needed = (key_pos[0] >= 0) & (key_pos[0] <= set_one[2][-1]) & (key_pos[-1] >= earliest)
            results.append(
                lax.cond(
                    needed,
                    lambda carried: attend_piece(
                        carried, set_one, key_part, key_req, key_pos, True
                    ),
                    lambda carried: carried,
                    state_one,
                )
            )
        else:
            results.append(attend_piece(state_one, set_one, key_part, key_req, key_pos, False))
    return tuple(results)


def empty_state(query_count, head_count, head_size):
    return (
        jnp.zeros((head_count, query_count, head_size), jnp.float32),
        jnp.full((head_count, query_count), neg_big, jnp.float32),
        jnp.zeros((head_count, query_count), jnp.float32),
    )


def finish_context(state_one):
    context_sum, row_max, row_total = state_one
    context = context_sum / row_total[..., None]
    return jnp.transpose(context, (1, 0, 2)).reshape(context.shape[1], -1).astype(jnp.bfloat16)


def local(
    tokens,
    lengths,
    owners,
    prefix_cache,
    routes,
    gates,
    attn_gain,
    w_query,
    w_keyval,
    w_out,
    moe_gain,
    w_gate,
    w_up,
    w_down,
    final_gain,
    unembed,
):
    tok_rows = tokens.shape[1]
    model_width = tokens.shape[2]
    head_count = HEADS
    head_size = w_query.shape[1] // head_count
    blocks = lax.axis_size("blk")
    block_index = lax.axis_index("blk")
    stream = tokens[0]
    normed = rms_scale(stream, attn_gain).astype(jnp.bfloat16)
    queries = jnp.dot(normed, w_query, preferred_element_type=jnp.float32).astype(jnp.bfloat16)
    suffix_kv = jnp.dot(normed, w_keyval, preferred_element_type=jnp.float32).astype(jnp.bfloat16)
    request_ends = jnp.cumsum(lengths[0])
    positions = block_index * tok_rows + jnp.arange(tok_rows, dtype=jnp.int32)
    requests = request_of(positions, request_ends)
    query_sets = ((queries, requests, positions),)
    states = tuple((empty_state(one[0].shape[0], head_count, head_size) for one in query_sets))
    owner_id = owners[0]
    blank_prefix = jnp.zeros_like(prefix_cache[0])
    arrived = lax.all_gather(prefix_cache, "grp", axis=0, tiled=True)
    first_row = jnp.int32(0)
    shard_count = arrived.shape[0]
    inside = (owner_id >= first_row) & (owner_id < first_row + shard_count)
    offset = jnp.clip(owner_id, 0, shard_count - 1)
    owner_prefix = jnp.where(
        inside, lax.dynamic_index_in_dim(arrived, offset, 0, keepdims=False), blank_prefix
    )
    states = fold_sets(
        states,
        query_sets,
        lax.all_gather(owner_prefix, "blk", axis=0, tiled=True),
        None,
        None,
        False,
        request_ends,
    )
    arrived = lax.all_gather(suffix_kv, "blk", axis=0, tiled=True)
    key_pos = jnp.arange(arrived.shape[0], dtype=jnp.int32)
    states = fold_sets(
        states, query_sets, arrived, request_of(key_pos, request_ends), key_pos, True, request_ends
    )
    contexts = [finish_context(one) for one in states]
    context = contexts[0]
    mixed_stream = stream.astype(jnp.float32) + jnp.dot(
        context, w_out, preferred_element_type=jnp.float32
    )
    routed_in = rms_scale(mixed_stream, moe_gain).astype(jnp.bfloat16)
    targets = slot_targets(routes[0])
    dispatch = dispatch_matrix(targets)
    packed = jnp.dot(dispatch, routed_in, preferred_element_type=jnp.float32).astype(jnp.bfloat16)
    split_count = blocks // EXPERTS
    outgoing = jnp.broadcast_to(
        packed.reshape(EXPERTS, 1, CAP, model_width), (EXPERTS, split_count, CAP, model_width)
    ).reshape(blocks, CAP, model_width)
    arrived = lax.all_to_all(outgoing, "blk", split_axis=0, concat_axis=0, tiled=True)
    flat_rows = arrived.reshape(-1, model_width)
    gate_value = jnp.dot(flat_rows, w_gate[0], preferred_element_type=jnp.float32)
    up_value = jnp.dot(flat_rows, w_up[0], preferred_element_type=jnp.float32)
    hidden = (jax.nn.gelu(gate_value, approximate=True) * up_value).astype(jnp.bfloat16)
    partial_value = (
        jnp.dot(hidden, w_down[0], preferred_element_type=jnp.float32)
        .astype(jnp.bfloat16)
        .reshape(arrived.shape)
    )
    returned_parts = lax.all_to_all(partial_value, "blk", split_axis=0, concat_axis=0, tiled=True)
    summed = jnp.sum(
        returned_parts.reshape(EXPERTS, split_count, CAP, model_width).astype(jnp.float32), axis=1
    ).reshape(EXPERTS * CAP, model_width)
    first_pick = jnp.take(summed, targets[:, 0], axis=0)
    second_pick = jnp.take(summed, targets[:, 1], axis=0)
    moe_out = gates[0][:, 0:1] * first_pick + gates[0][:, 1:2] * second_pick
    hidden_out = (mixed_stream + moe_out).astype(jnp.bfloat16)
    squares = jnp.sum(jnp.square(hidden_out.astype(jnp.float32)), axis=1)
    member = requests[:, None] == jnp.arange(lengths.shape[1], dtype=jnp.int32)[None, :]
    norm_terms = jnp.sum(jnp.where(member, squares[:, None], 0.0), axis=0)
    is_last = positions[:, None] == (request_ends - 1)[None, :]
    final_rows = rms_scale(hidden_out, final_gain).astype(jnp.bfloat16)
    last_terms = jnp.einsum(
        "tr,td->rd", is_last.astype(jnp.bfloat16), final_rows, preferred_element_type=jnp.float32
    )
    norm_sums, last_rows = (
        lax.psum(norm_terms.astype(jnp.bfloat16), "blk").astype(jnp.float32),
        lax.psum(last_terms.astype(jnp.bfloat16), "blk").astype(jnp.float32),
    )
    logits = jnp.dot(last_rows.astype(jnp.bfloat16), unembed, preferred_element_type=jnp.float32)
    greatest = lax.pmax(jnp.max(logits, axis=1), "blk")
    request_norm = jnp.sqrt(norm_sums / (lengths[0].astype(jnp.float32) * model_width))
    return (hidden_out[None], suffix_kv[None], request_norm[None], greatest[None])


def solution(mesh):
    placed = (
        P("grp", "blk", None),
        P("grp", None),
        P("grp"),
        P("grp", "blk", None),
        P("grp", "blk", None),
        P("grp", "blk", None),
        P(),
        P(),
        P(),
        P(),
        P(),
        P("blk", None, None),
        P("blk", None, None),
        P("blk", None, None),
        P(),
        P(None, "blk"),
    )
    return jax.shard_map(
        local,
        mesh=mesh,
        in_specs=placed,
        out_specs=(P("grp", "blk", None), P("grp", "blk", None), P("grp", None), P("grp", None)),
        check_vma=False,
    )
```

profile of v0, /device:TPU:1, one launch (start us, length us, event | category | flops | bytes accessed | tf_op | source)
XLA Modules:
  0.0 506.1 jit_solution(9666139919563082497)
XLA Ops:
  8.9 38.4 %all-gather.5.cloned.1.call-done = bf16[8,64,1024]{2,1,0:T(8,128)(2,1)} async-done(((bf16[1,64,1024]{2,1,0:T(8,128)(2,1)}), bf16[8,64,1024]{2,1,0:T(8,128)(2,1)}) %all-gather.5.cloned.1.call-update) | async-done | bytes 1048592 | tf_op jit(solution)/shard_map/all_gather | solution.py:146
  47.3 1.6 dynamic-slice_select_fusion
  49.0 1.1 fusion.37
  50.1 2.2 convolution_convert_fusion.2
  57.5 48.1 %all-gather.9.cloned.1.call-done = bf16[1,2048,1024]{2,1,0:T(8,128)(2,1)} async-done(((bf16[1,64,1024]{2,1,0:T(8,128)(2,1)}), bf16[1,2048,1024]{2,1,0:T(8,128)(2,1)}) %all-gather.9.cloned.1.call-update) | async-done | bytes 4194320 | tf_op jit(solution)/shard_map/all_gather | solution.py:157
  105.6 3.8 fusion.69
  109.4 2.5 copy.56
  111.9 2.9 copy.55
  114.8 1.4 multiply_reduce_fusion
  116.2 1.6 fusion.11
  117.9 1.9 fusion.29
  119.7 46.3 %all-gather.7.cloned.1.call-done = bf16[4096,1024]{1,0:T(8,128)(2,1)} async-done(((bf16[128,1024]{1,0:T(8,128)(2,1)}), bf16[4096,1024]{1,0:T(8,128)(2,1)}) %all-gather.7.cloned.1.call-update) | async-done | bytes 8388624 | tf_op jit(solution)/shard_map/all_gather | solution.py:163
  166.1 40.8 %conditional.1 = ((f32[8,128,64]{1,2,0:T(8,128)S(1)}, f32[8,128]{1,0:T(8,128)S(1)})) conditional(s32[]{:T(128)} %convert_element_type.95, (f32[8,128,64]{1,2,0:T(8,128)S(1)}, f32[8,128]{1,0:T(8,128)S(1)}) %tuple.16, (s32[128]{0:T(128)S(1)}, s32[4096,16]{0,1:T(8,128)S(1)}, s32[4096]{0:T(1024)S(1)}, s32[128]{0:T(128)S(1)}, ...), branch_computations={%region_5.6_spmd, %region_6.10_spmd} | conditional | flops 1121646592 | bytes 162767936 | solution.py:83
  166.3 11.4 %copy.58 = bf16[4096,1024]{0,1:T(8,128)(2,1)} copy(bf16[4096,1024]{1,0:T(8,128)(2,1)} %get-tuple-element.83) | data formatting | bytes 16777216 | tf_op jit(solution)/shard_map
  177.7 6.1 %fusion.68 = (bf16[4096,512]{0,1:T(8,128)(2,1)}, bf16[4096,512]{0,1:T(8,128)(2,1)}) fusion(bf16[4096,1024]{0,1:T(8,128)(2,1)} %copy.58), kind=kLoop, calls=%fused_computation.115 | loop fusion | bytes 16777216 | tf_op jit(solution)/shard_map/cond/branch_1_fun/slice | solution.py:51
  184.4 5.0 fusion
  189.4 4.8 fusion.1
  194.3 0.9 copy-done.2
  195.1 11.7 %fusion.6 = f32[8,128,64]{1,2,0:T(8,128)S(1)} fusion(bf16[4096,8,64]{0,2,1:T(8,128)(2,1)} %bitcast.90, f32[8,128,4096]{2,1,0:T(8,128)} %copy-done.2, f32[8,128]{1,0:T(8,128)S(1)} %max.12, pred[128,4096]{1,0:T(8,128)(4,1)S(1)} %compare_and_fusion, f32[8,128,64]{1,2,0:T(8,128)S(1)} %get-tuple-element.25, f32[8,128]{1,0:T(8,128)S(1)} %get-tuple-element.92), kind=kOutput, calls=%fused_computation.10 | convolution fusion | flops 553779200 | bytes 22028288 | tf_op jit(solution)/shard_map/cond/branch_1_fun/hqk,khd->hqd/dot_general | solution.py:66
  208.1 39.5 %all_to_all.10 = bf16[32,40,1024]{2,1,0:T(8,128)(2,1)S(1)} all-to-all(bf16[32,40,1024]{2,1,0:T(8,128)(2,1)S(1)} %bitcast.86), channel_id=1, replica_groups=mesh['grp'=8,'blk'=32] {'blk'}, dimensions={0} | all-to-all | bytes 5242880 | tf_op jit(solution)/shard_map/all_to_all | solution.py:181
  247.6 1.5 copy-done.6
  249.2 3.8 fusion.27
  253.0 9.7 %convolution_convert_fusion = bf16[1280,1024]{1,0:T(8,128)(2,1)} fusion(bf16[1,704,1024]{2,1,0:T(8,128)(2,1)S(1)} %copy-done.20, bf16[1280,1024]{1,0:T(8,128)(2,1)} %bitcast.93, f32[1280,704]{0,1:T(8,128)} %fusion.27, bf16[1,1024,704]{1,2,0:T(8,128)(2,1)} %param.32), kind=kOutput, calls=%fused_computation.25 | convolution fusion | flops 3701309440 | bytes 11730944 | tf_op jit(solution)/shard_map/dot_general | solution.py:187
  262.8 4.7 all-to-all-start.1
  267.6 33.5 %all-to-all-done.1 = bf16[32,40,1024]{2,1,0:T(8,128)(2,1)} async-done(((bf16[32,40,1024]{2,1,0:T(8,128)(2,1)}), bf16[32,40,1024]{2,1,0:T(8,128)(2,1)}, u32[]{:S(2)}, u32[]{:S(2)}) %all-to-all-start.1) | async-done | bytes 2621472 | tf_op jit(solution)/shard_map/all_to_all | solution.py:191
  301.1 2.4 convert_reduce_fusion
  303.5 1.6 gather_fusion.1
  305.0 1.6 gather_fusion
  306.6 1.7 fusion.34
  308.7 119.8 %all-reduce = (bf16[16]{0:T(256)(128)(2,1)S(1)}, bf16[16,1024]{1,0:T(8,128)(2,1)S(1)}) all-reduce(bf16[16]{0:T(256)(128)(2,1)S(1)} %select_reduce_fusion, bf16[16,1024]{1,0:T(8,128)(2,1)S(1)} %convolution_convert_fusion.4), channel_id=1, replica_groups=mesh['grp'=8,'blk'=32] {'blk'}, use_global_device_ids=true, to_apply=%region_17.19 | all-reduce | flops 16400 | bytes 65600 | tf_op jit(solution)/shard_map/psum | solution.py:208
  429.0 2.3 convolution_reduce_fusion
  431.4 68.2 %pmax.7 = f32[1,16]{1,0:T(1,128)} all-reduce(f32[1,16]{1,0:T(1,128)S(1)} %bitcast.101), channel_id=1, replica_groups=mesh['grp'=8,'blk'=32] {'blk'}, use_global_device_ids=true, to_apply=%region_20.22 | all-reduce | flops 16 | bytes 128 | tf_op jit(solution)/shard_map/pmax | solution.py:212
  (96 shorter events, 7.4 us)
Async XLA Ops:
  7.2 42.9 %copy-start = (bf16[1024,1024]{1,0:T(8,128)(2,1)S(1)}, bf16[1024,1024]{1,0:T(8,128)(2,1)}, u32[]{:S(2)}) copy-start(bf16[1024,1024]{1,0:T(8,128)(2,1)} %param.28) | copy-start | bytes 6291460
  7.2 48.3 %copy-start.5 = (bf16[1,128,1024]{2,1,0:T(8,128)(2,1)S(1)}, bf16[1,128,1024]{2,1,0:T(8,128)(2,1)}, u32[]{:S(2)}) copy-start(bf16[1,128,1024]{2,1,0:T(8,128)(2,1)} %param.20) | copy-start | bytes 786436
  7.2 48.3 %copy-start.10 = (f32[1024]{0:T(1024)S(1)}, f32[1024]{0:T(1024)}, u32[]{:S(2)}) copy-start(f32[1024]{0:T(1024)} %param.26) | copy-start | bytes 12292
  7.2 45.0 %copy-start.12 = (s32[1,128,2]{1,2,0:T(2,128)S(1)}, s32[1,128,2]{1,2,0:T(2,128)}, u32[]{:S(2)}) copy-start(s32[1,128,2]{1,2,0:T(2,128)} %param.24) | copy-start | bytes 3076
  7.2 46.7 %copy-start.14 = (s32[1,16]{1,0:T(1,128)S(1)}, s32[1,16]{1,0:T(1,128)}, u32[]{:S(2)}) copy-start(s32[1,16]{1,0:T(1,128)} %param.21) | copy-start | bytes 196
  7.2 48.3 %copy-start.7 = (bf16[1024,512]{1,0:T(8,128)(2,1)S(1)}, bf16[1024,512]{1,0:T(8,128)(2,1)}, u32[]{:S(2)}) copy-start(bf16[1024,512]{1,0:T(8,128)(2,1)} %param.27) | copy-start | bytes 3145732
  7.2 40.1 %all-gather.5.cloned.1.call-start = ((), (), s32[]{:S(2)}) async-start(), calls=%async_computation.2 | async-start | bytes 1179648 | tf_op jit(solution)/shard_map/all_gather | solution.py:146
  8.0 97.6 %all-gather.9.cloned.1.call-start = ((), (), s32[]{:S(2)}) async-start(), calls=%async_computation.4 | async-start | bytes 4325376 | tf_op jit(solution)/shard_map/all_gather | solution.py:157
  48.9 117.2 %all-gather.7.cloned.1.call-start = ((), (), s32[]{:S(2)}) async-start(), calls=%async_computation.3 | async-start | bytes 8650752 | tf_op jit(solution)/shard_map/all_gather | solution.py:163
  52.7 3.4 copy-start.15
  54.3 1.6 copy-start.17
  116.2 1.7 copy-start.3
  117.9 48.2 %copy-start.16 = (s32[128]{0:T(128)S(1)}, s32[128]{0:T(128)}, u32[]{:S(2)}) copy-start(s32[128]{0:T(128)} %copy-done.15) | copy-start | bytes 1540
  117.9 48.2 %copy-start.18 = (s32[128]{0:T(128)S(1)}, s32[128]{0:T(128)}, u32[]{:S(2)}) copy-start(s32[128]{0:T(128)} %copy-done.17) | copy-start | bytes 1540
  166.1 40.8 %copy-start.8 = (bf16[512,1024]{1,0:T(8,128)(2,1)S(1)}, bf16[512,1024]{1,0:T(8,128)(2,1)}, u32[]{:S(2)}) copy-start(bf16[512,1024]{1,0:T(8,128)(2,1)} %param.29) | copy-start | bytes 3145732
  166.1 41.3 %copy-start.11 = (f32[1024]{0:T(1024)S(1)}, f32[1024]{0:T(1024)}, u32[]{:S(2)}) copy-start(f32[1024]{0:T(1024)} %param.30) | copy-start | bytes 12292
  189.4 5.7 %copy-start.2 = (f32[8,128,4096]{2,1,0:T(8,128)}, f32[8,128,4096]{2,1,0:T(8,128)S(1)}, u32[]{:S(2)}) copy-start(f32[8,128,4096]{2,1,0:T(8,128)S(1)} %get-tuple-element.98) | copy-start | bytes 50331652 | tf_op jit(solution)/shard_map/cond
  207.3 40.3 %copy-start.4 = (f32[128,1024]{1,0:T(8,128)}, f32[128,1024]{1,0:T(8,128)S(1)}, u32[]{:S(2)}) copy-start(f32[128,1024]{1,0:T(8,128)S(1)} %get-tuple-element.108) | copy-start | bytes 1572868
  207.8 41.4 %copy-start.19 = (bf16[1,1024,704]{1,2,0:T(8,128)(2,1)S(1)}, bf16[1,1024,704]{1,2,0:T(8,128)(2,1)}, u32[]{:S(2)}) copy-start(bf16[1,1024,704]{1,2,0:T(8,128)(2,1)} %param.31) | copy-start | bytes 4325380
  247.6 1.5 copy-start.6
  249.2 3.8 copy-start.20
  262.8 4.8 copy-start.13
  262.8 38.3 %all-to-all-start.1 = ((bf16[32,40,1024]{2,1,0:T(8,128)(2,1)}), bf16[32,40,1024]{2,1,0:T(8,128)(2,1)}, u32[]{:S(2)}, u32[]{:S(2)}) async-start(bf16[32,40,1024]{2,1,0:T(8,128)(2,1)} %bitcast.91), calls=%async_computation.1 | async-start | bytes 5242880 | tf_op jit(solution)/shard_map/all_to_all | solution.py:191
  303.5 196.1 %copy-start.1 = (bf16[1024,1024]{1,0:T(8,128)(2,1)S(1)}, bf16[1024,1024]{1,0:T(8,128)(2,1)}, u32[]{:S(2)}) copy-start(bf16[1024,1024]{1,0:T(8,128)(2,1)} %param.28) | copy-start | bytes 6291460
  305.0 3.3 copy-start.21
  308.3 191.2 %copy-start.9 = (bf16[128,1024]{1,0:T(8,128)(2,1)}, bf16[128,1024]{1,0:T(8,128)(2,1)S(1)}, u32[]{:S(2)}) copy-start(bf16[128,1024]{1,0:T(8,128)(2,1)S(1)} %get-tuple-element.94) | copy-start | bytes 786436
Sparse Core Ops, SparseCore 0:
  9.9 37.4 all-gather.4
  50.5 55.0 all-gather.8
  108.7 57.3 all-gather.6
where the time goes:
time: 507 us; the launch traced here: 506 us
  blocking collectives  227 us (45%)
  waiting for transfers between devices  167 us (33%)
  matrix products  39.4 us (8%)
  local copies, waits for them, and re-layouts  35.1 us (7%)
  between operations  16.4 us (3%)
  other arithmetic  15.5 us (3%)
    psum x1, blocking collectives, local(): lax.psum(norm_terms.astype(jnp.bfloat16), 'blk').astype(jnp.float32)  120 us
    pmax x1, blocking collectives, local(): greatest = lax.pmax(jnp.max(logits, axis=1), 'blk')  68.2 us
    all_gather x1, waiting for transfers between devices, local(): lax.all_gather(owner_prefix, 'blk', axis=0, tiled=True)  48.1 us
    all_gather x1, waiting for transfers between devices, local(): arrived = lax.all_gather(suffix_kv, 'blk', axis=0, tiled=True)  46.3 us
    all_to_all x1, blocking collectives, local(): lax.all_to_all(outgoing, 'blk', split_axis=0, concat_axis=0, tiled=True)  39.5 us
    all_gather x1, waiting for transfers between devices, local(): arrived = lax.all_gather(prefix_cache, 'grp', axis=0, tiled=True)  38.4 us
    all_to_all x1, waiting for transfers between devices, local(): lax.all_to_all(partial_value, 'blk', split_axis=0, concat_axis=0, tiled=T...  33.5 us
    dot_general x2, matrix products, attend_piece(): jnp.einsum('hqk,khd->hqd', probs_full.astype(jnp.bfloat16), value_heads,...  13.6 us
  transfers between devices with their start and end apart: 4, of which 4 were waited for; matrix products, arithmetic and copies ran while one was open for 4% of the time, Pallas kernels for 0%

commit v1 on v0

--- a/solution.py
+++ b/solution.py
@@ -8,6 +8,38 @@
 CAP = 40
 epsilon = 1e-06
 neg_big = -1e30
+
+
+def sector_see(work_x, where_dim):
+    work_x = jnp.moveaxis(work_x, 0, where_dim)
+    block_out = work_x.shape
+    return work_x.reshape(
+        *block_out[:where_dim],
+        block_out[where_dim] * block_out[where_dim + 1],
+        *block_out[where_dim + 2 :]
+    )
+
+
+def begin_the_waves(local_x, net_axis, in_dim):
+    shares = lax.axis_size(net_axis)
+    inbox = [(u, (u + 1) % shares) for u in range(shares)]
+    vals = [(ix, idx) for idx, ix in inbox]
+    side_arr, kept_arr = ([], [])
+    dev_j = 0
+    while dev_j < shares - 1:
+        if dev_j % 2 == 0:
+            next_value = lax.ppermute(side_arr[-1] if side_arr else local_x, net_axis, perm=inbox)
+            side_arr.append(next_value)
+        else:
+            current_value = lax.ppermute(kept_arr[-1] if kept_arr else local_x, net_axis, perm=vals)
+            kept_arr.append(current_value)
+        dev_j += 1
+    current_arr = jnp.stack([*side_arr[::-1], local_x, *kept_arr], axis=0)
+    v1 = lax.axis_index(net_axis)
+    all_values = len(side_arr)
+    w2 = v1 - all_values
+    current_arr = current_arr[(jnp.arange(shares) - w2) % shares]
+    return sector_see(current_arr, in_dim)
 
 
 def rms_scale(values, gain_vector):
@@ -143,7 +175,7 @@
     states = tuple((empty_state(one[0].shape[0], head_count, head_size) for one in query_sets))
     owner_id = owners[0]
     blank_prefix = jnp.zeros_like(prefix_cache[0])
-    arrived = lax.all_gather(prefix_cache, "grp", axis=0, tiled=True)
+    arrived = begin_the_waves(prefix_cache, "grp", 0)
     first_row = jnp.int32(0)
     shard_count = arrived.shape[0]
     inside = (owner_id >= first_row) & (owner_id < first_row + shard_count)

time: 507 us -> 494 us (0.974)
  waiting for transfers between devices: 167 us -> 143 us
  starting transfers between devices: 4.83 us -> 15.8 us
    all_gather x1 -> x0, waiting for transfers between devices: 38.4 us -> none  [local(): arrived = lax.all_gather(prefix_cache, 'grp', axis=0, tiled=True)]
    ppermute x0 -> x7, waiting for transfers between devices: none -> 13.5 us  [the longest x4 13.4 us: begin_the_waves(): lax.ppermute(side_arr[-1] if side_arr else local_x, net_axis, perm=inbox)]
    ppermute x0 -> x7, starting transfers between devices: none -> 10.9 us  [the longest x3 8.3 us: begin_the_waves(): lax.ppermute(kept_arr[-1] if kept_arr else local_x, net_axis, perm=vals)]
    another operation x3 -> x4, local copies, waits for them, and re-layouts: 11.5 us -> 11.5 us
  transfers between devices with their start and end apart: 4 -> 10, of which waited for: 4 -> 7; matrix products, arithmetic and copies ran while one was open for 4% -> 4% of each run, Pallas kernels for 0% -> 0%
where the time goes in v1:
time: 494 us
  blocking collectives  227 us (46%)
  waiting for transfers between devices  143 us (29%)
  local copies, waits for them, and re-layouts  38.9 us (8%)
  matrix products  38.5 us (8%)
  between operations  16.6 us (3%)
  starting transfers between devices  15.8 us (3%)
  other arithmetic  13.6 us (3%)
    psum x1, blocking collectives, local(): lax.psum(norm_terms.astype(jnp.bfloat16), 'blk').astype(jnp.float32)  120 us
    pmax x1, blocking collectives, local(): greatest = lax.pmax(jnp.max(logits, axis=1), 'blk')  68.2 us
    all_gather x1, waiting for transfers between devices, local(): lax.all_gather(owner_prefix, 'blk', axis=0, tiled=True)  49.2 us
    all_gather x1, waiting for transfers between devices, local(): arrived = lax.all_gather(suffix_kv, 'blk', axis=0, tiled=True)  46.3 us
    all_to_all x1, blocking collectives, local(): lax.all_to_all(outgoing, 'blk', split_axis=0, concat_axis=0, tiled=True)  39.5 us
    all_to_all x1, waiting for transfers between devices, local(): lax.all_to_all(partial_value, 'blk', split_axis=0, concat_axis=0, tiled=T...  33.5 us
    dot_general x2, matrix products, attend_piece(): jnp.einsum('hqk,khd->hqd', probs_full.astype(jnp.bfloat16), value_heads,...  13.6 us
    ppermute x4, waiting for transfers between devices, begin_the_waves(): lax.ppermute(side_arr[-1] if side_arr else local_x, net_axis, perm=inbox)  13.4 us
  transfers between devices with their start and end apart: 10, of which 7 were waited for; matrix products, arithmetic and copies ran while one was open for 4% of the time, Pallas kernels for 0%

profile of v1, /device:TPU:1, one launch (start us, length us, event | category | flops | bytes accessed | tf_op | source)
XLA Modules:
  0.0 493.7 jit_solution(16223565296967269438)
XLA Ops:
  7.2 2.5 collective-permute-start
  9.8 7.4 %collective-permute-done = bf16[1,64,1024]{2,1,0:T(8,128)(2,1)S(1)} collective-permute-done((bf16[1,64,1024]{2,1,0:T(8,128)(2,1)}, bf16[1,64,1024]{2,1,0:T(8,128)(2,1)S(1)}, u32[]{:S(2)}, u32[]{:S(2)}) %collective-permute-start) | collective-permute-done | bytes 131104 | tf_op jit(solution)/shard_map/ppermute | solution.py:31
  17.2 2.7 collective-permute-start.4
  19.8 2.4 collective-permute-done.1
  22.2 2.9 collective-permute-start.5
  25.1 2.1 collective-permute-done.2
  27.9 2.7 collective-permute-start.6
  34.3 1.8 gather_fusion
  43.7 49.2 %all-gather.7.cloned.1.call-done = bf16[1,2048,1024]{2,1,0:T(8,128)(2,1)} async-done(((bf16[1,64,1024]{2,1,0:T(8,128)(2,1)}), bf16[1,2048,1024]{2,1,0:T(8,128)(2,1)}) %all-gather.7.cloned.1.call-update) | async-done | bytes 4194320 | tf_op jit(solution)/shard_map/all_gather | solution.py:189
  92.9 3.8 fusion.71
  96.7 2.5 copy.47
  99.2 2.9 copy.46
  103.5 1.6 fusion.11
  105.2 1.9 fusion.29
  107.0 46.3 %all-gather.5.cloned.1.call-done = bf16[4096,1024]{1,0:T(8,128)(2,1)} async-done(((bf16[128,1024]{1,0:T(8,128)(2,1)}), bf16[4096,1024]{1,0:T(8,128)(2,1)}) %all-gather.5.cloned.1.call-update) | async-done | bytes 8388624 | tf_op jit(solution)/shard_map/all_gather | solution.py:195
  153.4 40.8 %conditional.1 = ((f32[8,128,64]{1,2,0:T(8,128)S(1)}, f32[8,128]{1,0:T(8,128)S(1)})) conditional(s32[]{:T(128)} %convert_element_type.95, (f32[8,128,64]{1,2,0:T(8,128)S(1)}, f32[8,128]{1,0:T(8,128)S(1)}) %tuple.16, (s32[128]{0:T(128)S(1)}, s32[4096,16]{0,1:T(8,128)S(1)}, s32[4096]{0:T(1024)S(1)}, s32[128]{0:T(128)S(1)}, ...), branch_computations={%region_5.6_spmd, %region_6.10_spmd} | conditional | flops 1121646592 | bytes 162767936 | solution.py:115
  153.6 11.3 %copy.49 = bf16[4096,1024]{0,1:T(8,128)(2,1)} copy(bf16[4096,1024]{1,0:T(8,128)(2,1)} %get-tuple-element.74) | data formatting | bytes 16777216 | tf_op jit(solution)/shard_map
  165.0 6.1 %fusion.70 = (bf16[4096,512]{0,1:T(8,128)(2,1)}, bf16[4096,512]{0,1:T(8,128)(2,1)}) fusion(bf16[4096,1024]{0,1:T(8,128)(2,1)} %copy.49), kind=kLoop, calls=%fused_computation.131 | loop fusion | bytes 16777216 | tf_op jit(solution)/shard_map/cond/branch_1_fun/slice | solution.py:83
  171.7 5.0 %fusion = (f32[8,128]{1,0:T(8,128)S(1)}, f32[8,128,4096]{2,1,0:T(8,128)S(1)}) fusion(pred[128,4096]{1,0:T(8,128)(4,1)S(1)} %compare_and_fusion, bf16[128,8,64]{0,2,1:T(8,128)(2,1)S(1)} %bitcast.116, bf16[4096,8,64]{0,2,1:T(8,128)(2,1)} %bitcast.104), kind=kOutput, calls=%fused_computation.5 | convolution fusion | flops 549452800 | bytes 21630976 | tf_op jit(solution)/shard_map/cond/branch_1_fun/qhd,khd->hqk/dot_general | solution.py:86
  176.7 4.8 fusion.1
  182.4 11.7 %fusion.6 = f32[8,128,64]{1,2,0:T(8,128)S(1)} fusion(bf16[4096,8,64]{0,2,1:T(8,128)(2,1)} %bitcast.109, f32[8,128,4096]{2,1,0:T(8,128)} %copy-done.2, f32[8,128]{1,0:T(8,128)S(1)} %max.12, pred[128,4096]{1,0:T(8,128)(4,1)S(1)} %compare_and_fusion, f32[8,128,64]{1,2,0:T(8,128)S(1)} %get-tuple-element.25, f32[8,128]{1,0:T(8,128)S(1)} %get-tuple-element.83), kind=kOutput, calls=%fused_computation.11 | convolution fusion | flops 553779200 | bytes 22028288 | tf_op jit(solution)/shard_map/cond/branch_1_fun/hqk,khd->hqd/dot_general | solution.py:98
  195.4 39.5 %all_to_all.10 = bf16[32,40,1024]{2,1,0:T(8,128)(2,1)S(1)} all-to-all(bf16[32,40,1024]{2,1,0:T(8,128)(2,1)S(1)} %bitcast.105), channel_id=1, replica_groups=mesh['grp'=8,'blk'=32] {'blk'}, dimensions={0} | all-to-all | bytes 5242880 | tf_op jit(solution)/shard_map/all_to_all | solution.py:213
  236.5 3.8 fusion.27
  240.3 9.7 %convolution_convert_fusion = bf16[1280,1024]{1,0:T(8,128)(2,1)} fusion(bf16[1,704,1024]{2,1,0:T(8,128)(2,1)S(1)} %copy-done.21, bf16[1280,1024]{1,0:T(8,128)(2,1)} %bitcast.112, f32[1280,704]{0,1:T(8,128)} %fusion.27, bf16[1,1024,704]{1,2,0:T(8,128)(2,1)} %param.32), kind=kOutput, calls=%fused_computation.26 | convolution fusion | flops 3701309440 | bytes 11730944 | tf_op jit(solution)/shard_map/dot_general | solution.py:219
  250.1 4.7 all-to-all-start.1
  254.9 33.5 %all-to-all-done.1 = bf16[32,40,1024]{2,1,0:T(8,128)(2,1)} async-done(((bf16[32,40,1024]{2,1,0:T(8,128)(2,1)}), bf16[32,40,1024]{2,1,0:T(8,128)(2,1)}, u32[]{:S(2)}, u32[]{:S(2)}) %all-to-all-start.1) | async-done | bytes 2621472 | tf_op jit(solution)/shard_map/all_to_all | solution.py:223
  288.4 2.4 convert_reduce_fusion
  292.3 1.6 gather_fusion.1
  293.9 1.7 fusion.34
  296.0 119.8 %all-reduce = (bf16[16]{0:T(256)(128)(2,1)S(1)}, bf16[16,1024]{1,0:T(8,128)(2,1)S(1)}) all-reduce(bf16[16]{0:T(256)(128)(2,1)S(1)} %select_reduce_fusion, bf16[16,1024]{1,0:T(8,128)(2,1)S(1)} %convolution_convert_fusion.4), channel_id=1, replica_groups=mesh['grp'=8,'blk'=32] {'blk'}, use_global_device_ids=true, to_apply=%region_17.19 | all-reduce | flops 16400 | bytes 65600 | tf_op jit(solution)/shard_map/psum | solution.py:240
  416.3 2.3 convolution_reduce_fusion
  418.6 68.2 %pmax.7 = f32[1,16]{1,0:T(1,128)} all-reduce(f32[1,16]{1,0:T(1,128)S(1)} %bitcast.121), channel_id=1, replica_groups=mesh['grp'=8,'blk'=32] {'blk'}, use_global_device_ids=true, to_apply=%region_20.22 | all-reduce | flops 16 | bytes 128 | tf_op jit(solution)/shard_map/pmax | solution.py:244
  (120 shorter events, 17.8 us)
Async XLA Ops:
  7.2 30.1 %copy-start = (bf16[1024,1024]{1,0:T(8,128)(2,1)S(1)}, bf16[1024,1024]{1,0:T(8,128)(2,1)}, u32[]{:S(2)}) copy-start(bf16[1024,1024]{1,0:T(8,128)(2,1)} %param.28) | copy-start | bytes 6291460
  7.2 29.9 %copy-start.5 = (bf16[1,128,1024]{2,1,0:T(8,128)(2,1)S(1)}, bf16[1,128,1024]{2,1,0:T(8,128)(2,1)}, u32[]{:S(2)}) copy-start(bf16[1,128,1024]{2,1,0:T(8,128)(2,1)} %param.20) | copy-start | bytes 786436
  7.2 30.1 %copy-start.11 = (f32[1024]{0:T(1024)S(1)}, f32[1024]{0:T(1024)}, u32[]{:S(2)}) copy-start(f32[1024]{0:T(1024)} %param.26) | copy-start | bytes 12292
  7.2 85.7 %all-gather.7.cloned.1.call-start = ((), (), s32[]{:S(2)}) async-start(), calls=%async_computation.3 | async-start | bytes 4325376 | tf_op jit(solution)/shard_map/all_gather | solution.py:189
  7.2 9.9 %collective-permute-start = (bf16[1,64,1024]{2,1,0:T(8,128)(2,1)}, bf16[1,64,1024]{2,1,0:T(8,128)(2,1)S(1)}, u32[]{:S(2)}, u32[]{:S(2)}) collective-permute-start(bf16[1,64,1024]{2,1,0:T(8,128)(2,1)} %param.23), channel_id=1, source_target_pairs={{0,32},{32,64},{64,96},{96,128},{128,160},{160,192},{192,224},{224... | collective-permute-start | bytes 393224 | tf_op jit(solution)/shard_map/ppermute | solution.py:31
  17.2 5.0 %collective-permute-start.1 = (bf16[1,64,1024]{2,1,0:T(8,128)(2,1)S(1)}, bf16[1,64,1024]{2,1,0:T(8,128)(2,1)S(1)}, u32[]{:S(2)}, u32[]{:S(2)}) collective-permute-start(bf16[1,64,1024]{2,1,0:T(8,128)(2,1)S(1)} %collective-permute-done), channel_id=1, source_target_pairs={{0,32},{32,64},{64,96},{96,128},{128,160},{160,192},{192,224},{224... | collective-permute-start | bytes 393224 | tf_op jit(solution)/shard_map/ppermute | solution.py:31
  17.2 5.0 %collective-permute-start.4 = (bf16[1,64,1024]{2,1,0:T(8,128)(2,1)}, bf16[1,64,1024]{2,1,0:T(8,128)(2,1)S(1)}, u32[]{:S(2)}, u32[]{:S(2)}) collective-permute-start(bf16[1,64,1024]{2,1,0:T(8,128)(2,1)} %param.23), channel_id=1, source_target_pairs={{32,0},{64,32},{96,64},{128,96},{160,128},{192,160},{224,192},{0,2... | collective-permute-start | bytes 393224 | tf_op jit(solution)/shard_map/ppermute | solution.py:34
  22.2 5.0 %collective-permute-start.2 = (bf16[1,64,1024]{2,1,0:T(8,128)(2,1)S(1)}, bf16[1,64,1024]{2,1,0:T(8,128)(2,1)S(1)}, u32[]{:S(2)}, u32[]{:S(2)}) collective-permute-start(bf16[1,64,1024]{2,1,0:T(8,128)(2,1)S(1)} %collective-permute-done.1), channel_id=1, source_target_pairs={{0,32},{32,64},{64,96},{96,128},{128,160},{160,192},{192,224},{224... | collective-permute-start | bytes 393224 | tf_op jit(solution)/shard_map/ppermute | solution.py:31
  22.2 5.7 %collective-permute-start.5 = (bf16[1,64,1024]{2,1,0:T(8,128)(2,1)S(1)}, bf16[1,64,1024]{2,1,0:T(8,128)(2,1)S(1)}, u32[]{:S(2)}, u32[]{:S(2)}) collective-permute-start(bf16[1,64,1024]{2,1,0:T(8,128)(2,1)S(1)} %collective-permute-done.4), channel_id=1, source_target_pairs={{32,0},{64,32},{96,64},{128,96},{160,128},{192,160},{224,192},{0,2... | collective-permute-start | bytes 393224 | tf_op jit(solution)/shard_map/ppermute | solution.py:34
  27.2 5.0 %collective-permute-start.3 = (bf16[1,64,1024]{2,1,0:T(8,128)(2,1)S(1)}, bf16[1,64,1024]{2,1,0:T(8,128)(2,1)S(1)}, u32[]{:S(2)}, u32[]{:S(2)}) collective-permute-start(bf16[1,64,1024]{2,1,0:T(8,128)(2,1)S(1)} %collective-permute-done.2), channel_id=1, source_target_pairs={{0,32},{32,64},{64,96},{96,128},{128,160},{160,192},{192,224},{224... | collective-permute-start | bytes 393224 | tf_op jit(solution)/shard_map/ppermute | solution.py:31
  27.9 5.4 %collective-permute-start.6 = (bf16[1,64,1024]{2,1,0:T(8,128)(2,1)S(1)}, bf16[1,64,1024]{2,1,0:T(8,128)(2,1)S(1)}, u32[]{:S(2)}, u32[]{:S(2)}) collective-permute-start(bf16[1,64,1024]{2,1,0:T(8,128)(2,1)S(1)} %collective-permute-done.5), channel_id=1, source_target_pairs={{32,0},{64,32},{96,64},{128,96},{160,128},{192,160},{224,192},{0,2... | collective-permute-start | bytes 393224 | tf_op jit(solution)/shard_map/ppermute | solution.py:34
  32.3 6.2 %copy-start.13 = (s32[1,128,2]{1,2,0:T(2,128)S(1)}, s32[1,128,2]{1,2,0:T(2,128)}, u32[]{:S(2)}) copy-start(s32[1,128,2]{1,2,0:T(2,128)} %param.24) | copy-start | bytes 3076
  32.3 7.9 %copy-start.15 = (s32[1,16]{1,0:T(1,128)S(1)}, s32[1,16]{1,0:T(1,128)}, u32[]{:S(2)}) copy-start(s32[1,16]{1,0:T(1,128)} %param.21) | copy-start | bytes 196
  36.8 4.9 copy-start.8
  36.9 116.5 %all-gather.5.cloned.1.call-start = ((), (), s32[]{:S(2)}) async-start(), calls=%async_computation.2 | async-start | bytes 8650752 | tf_op jit(solution)/shard_map/all_gather | solution.py:195
  38.9 3.4 copy-start.16
  40.5 1.6 copy-start.18
  103.5 1.7 copy-start.3
  105.2 48.2 %copy-start.17 = (s32[128]{0:T(128)S(1)}, s32[128]{0:T(128)}, u32[]{:S(2)}) copy-start(s32[128]{0:T(128)} %copy-done.16) | copy-start | bytes 1540
  105.2 48.2 %copy-start.19 = (s32[128]{0:T(128)S(1)}, s32[128]{0:T(128)}, u32[]{:S(2)}) copy-start(s32[128]{0:T(128)} %copy-done.18) | copy-start | bytes 1540
  153.4 40.8 %copy-start.9 = (bf16[512,1024]{1,0:T(8,128)(2,1)S(1)}, bf16[512,1024]{1,0:T(8,128)(2,1)}, u32[]{:S(2)}) copy-start(bf16[512,1024]{1,0:T(8,128)(2,1)} %param.29) | copy-start | bytes 3145732
  153.4 41.3 %copy-start.12 = (f32[1024]{0:T(1024)S(1)}, f32[1024]{0:T(1024)}, u32[]{:S(2)}) copy-start(f32[1024]{0:T(1024)} %param.30) | copy-start | bytes 12292
  176.7 5.7 %copy-start.2 = (f32[8,128,4096]{2,1,0:T(8,128)}, f32[8,128,4096]{2,1,0:T(8,128)S(1)}, u32[]{:S(2)}) copy-start(f32[8,128,4096]{2,1,0:T(8,128)S(1)} %get-tuple-element.89) | copy-start | bytes 50331652 | tf_op jit(solution)/shard_map/cond
  194.6 40.3 %copy-start.4 = (f32[128,1024]{1,0:T(8,128)}, f32[128,1024]{1,0:T(8,128)S(1)}, u32[]{:S(2)}) copy-start(f32[128,1024]{1,0:T(8,128)S(1)} %get-tuple-element.99) | copy-start | bytes 1572868
  195.1 41.4 %copy-start.20 = (bf16[1,1024,704]{1,2,0:T(8,128)(2,1)S(1)}, bf16[1,1024,704]{1,2,0:T(8,128)(2,1)}, u32[]{:S(2)}) copy-start(bf16[1,1024,704]{1,2,0:T(8,128)(2,1)} %param.31) | copy-start | bytes 4325380
  234.9 1.5 copy-start.6
  236.5 3.8 copy-start.21
  250.1 4.8 copy-start.14
  250.1 38.3 %all-to-all-start.1 = ((bf16[32,40,1024]{2,1,0:T(8,128)(2,1)}), bf16[32,40,1024]{2,1,0:T(8,128)(2,1)}, u32[]{:S(2)}, u32[]{:S(2)}) async-start(bf16[32,40,1024]{2,1,0:T(8,128)(2,1)} %bitcast.110), calls=%async_computation.1 | async-start | bytes 5242880 | tf_op jit(solution)/shard_map/all_to_all | solution.py:223
  292.3 3.3 copy-start.22
  292.3 194.5 %copy-start.1 = (bf16[1024,1024]{1,0:T(8,128)(2,1)S(1)}, bf16[1024,1024]{1,0:T(8,128)(2,1)}, u32[]{:S(2)}) copy-start(bf16[1024,1024]{1,0:T(8,128)(2,1)} %param.28) | copy-start | bytes 6291460
  295.6 191.2 %copy-start.10 = (bf16[128,1024]{1,0:T(8,128)(2,1)}, bf16[128,1024]{1,0:T(8,128)(2,1)S(1)}, u32[]{:S(2)}) copy-start(bf16[128,1024]{1,0:T(8,128)(2,1)S(1)} %get-tuple-element.85) | copy-start | bytes 786436
  (1 other events, 1.0 us)
Sparse Core Ops, SparseCore 0:
  37.0 55.8 all-gather.6
  96.0 57.3 all-gather.4
